TPU v7x, 256 devices: a whole 4x4x8 slice. The times are simulated.
256 devices in a mesh: seq: 32 (over x, z_lo, core), dp: 8 (over z_hi, y).
Axes of the slice: x: 4, y: 4, z: 8 (z_hi: 2, z_lo: 4; z = z_hi * 4 + z_lo), core: 2. Of those that a mesh axis runs over, the one named last changes fastest.
Arguments:
- tokens: bfloat16 [8, 16384, 1536], P('dp', 'seq'), may hold values from -6 to 6
- cotangent: bfloat16 [8, 16384, 1536], P('dp', 'seq'), may hold values from -6 to 6
- conv_weight: float32 [3, 1536], replicated, may hold values from -3.5 to 3.5
- gate_weight: bfloat16 [1536, 1536], P('seq'), may hold values from -0.15625 to 0.15625
- leading_block_factor: bfloat16 [128, 128, 128], P('seq'), may hold values from -0.5 to 0.5
- trailing_block_factor: bfloat16 [128, 128, 128], P('seq'), may hold values from -0.5 to 0.5
Outputs:
- mixed: bfloat16 [8, 16384, 1536], P('dp', 'seq')
- grad_tokens: bfloat16 [8, 16384, 1536], P('dp', 'seq')
- grad_conv: float32 [3, 1536], replicated
- grad_gate: float32 [1536, 1536], P('seq')
- grad_first: float32 [128, 128, 128], P('seq')
- trailing_factor_gradient: float32 [128, 128, 128], P('seq')
All inputs are finite; a program needn't handle non-finite values.
Results may differ from a plain program's by a relative error of at most 0.0067.
Values may be sent and summed in bfloat16 or wider, within the bound.
No kernel may reach another device: no remote copies, remote signals or barrier semaphores. Data moves between devices by JAX's collectives and lax.ppermute only.
A program may use at most 128 MiB of HBM per device.

v0:
```python
import jax
import jax.numpy as jnp
from jax import lax
from jax.sharding import PartitionSpec as P


def with_halo(array, sides, width):
    for axis, dim in sides:
        count, length = (lax.axis_size(axis), array.shape[dim])
        up = [(i, (i + 1) % count) for i in range(count - 1)]
        down = [(j, i) for i, j in up]
        last = lax.slice_in_dim(array, length - width, length, axis=dim)
        first = lax.slice_in_dim(array, 0, width, axis=dim)
        before = lax.ppermute(last, axis, up)
        after = lax.ppermute(first, axis, down)
        array = jnp.concatenate([before, array, after], axis=dim)
    return array


def extend(values):
    return with_halo(values, (("seq", 0),), 1)


def regroup(values):
    return lax.all_to_all(values, "seq", split_axis=0, concat_axis=1, tiled=True)


def shards(
    tokens, cotangent, conv_weight, gate_weight, leading_block_factor, trailing_block_factor
):
    features = tokens[0]
    grad_out = cotangent[0]
    tok_rows = features.shape[0]
    feat_width = features.shape[1]
    local_blocks = leading_block_factor.shape[0]
    block_size = leading_block_factor.shape[1]
    feat_wide = features.astype(jnp.float32)
    pad_feat = extend(features).astype(jnp.float32)
    conv_in = (
        conv_weight[0] * pad_feat[:-2] + conv_weight[1] * feat_wide + conv_weight[2] * pad_feat[2:]
    ).astype(jnp.bfloat16)
    convolution_block_list = conv_in.reshape(local_blocks, block_size, feat_width)
    leading_output = jnp.einsum(
        "shz,szy->hsy",
        leading_block_factor,
        convolution_block_list,
        preferred_element_type=jnp.float32,
    ).astype(jnp.bfloat16)
    column_layout = regroup(leading_output)
    trailing_output = jnp.einsum(
        "vpn,vnu->pvu", trailing_block_factor, column_layout, preferred_element_type=jnp.float32
    ).astype(jnp.bfloat16)
    monarch = regroup(trailing_output).reshape(tok_rows, feat_width)
    whole_gate = lax.all_gather(gate_weight, "seq", axis=0, tiled=True)
    gate_act = jnp.dot(features, whole_gate, preferred_element_type=jnp.float32)
    mon_wide = monarch.astype(jnp.float32)
    grad_wide = grad_out.astype(jnp.float32)
    mixed = (mon_wide * gate_act).astype(jnp.bfloat16)
    d_monarch = (grad_wide * gate_act).astype(jnp.bfloat16)
    d_gate = (grad_wide * mon_wide).astype(jnp.bfloat16)
    second_factor_delta = lax.all_to_all(
        d_monarch.reshape(local_blocks, block_size, feat_width),
        "seq",
        split_axis=1,
        concat_axis=0,
        tiled=True,
    )
    d_inner = jnp.einsum(
        "ica,cid->aid",
        trailing_block_factor,
        second_factor_delta,
        preferred_element_type=jnp.float32,
    ).astype(jnp.bfloat16)
    trailing_factor_gradient = jnp.einsum(
        "wxn,xon->xwo", second_factor_delta, column_layout, preferred_element_type=jnp.float32
    )
    d_first = regroup(d_inner)
    d_conv = (
        jnp.einsum(
            "aib,aid->abd", leading_block_factor, d_first, preferred_element_type=jnp.float32
        )
        .astype(jnp.bfloat16)
        .reshape(tok_rows, feat_width)
    )
    grad_first = jnp.einsum(
        "aid,abd->aib", d_first, convolution_block_list, preferred_element_type=jnp.float32
    )
    d_convw = d_conv.astype(jnp.float32)
    conv_part = jnp.stack(
        [
            jnp.sum(d_convw * pad_feat[:-2], axis=0),
            jnp.sum(d_convw * feat_wide, axis=0),
            jnp.sum(d_convw * pad_feat[2:], axis=0),
        ]
    )
    pad_grad = extend(d_conv).astype(jnp.float32)
    conv_back = (
        conv_weight[0] * pad_grad[2:] + conv_weight[1] * d_convw + conv_weight[2] * pad_grad[:-2]
    )
    gate_back = lax.dot_general(
        d_gate, whole_gate, (((1,), (1,)), ((), ())), preferred_element_type=jnp.float32
    )
    grad_tokens = (conv_back + gate_back).astype(jnp.bfloat16)
    weight_part = lax.psum_scatter(
        lax.dot_general(
            features, d_gate, (((0,), (0,)), ((), ())), preferred_element_type=jnp.float32
        ),
        "seq",
        scatter_dimension=0,
        tiled=True,
    )
    grad_first, trailing_factor_gradient = lax.psum((grad_first, trailing_factor_gradient), "dp")
    grad_gate = lax.psum(weight_part, "dp")
    grad_conv = lax.psum(conv_part, ("seq", "dp"))
    return (
        mixed[None],
        grad_tokens[None],
        grad_conv,
        grad_gate,
        grad_first,
        trailing_factor_gradient,
    )


def solution(mesh):
    return jax.shard_map(
        shards,
        mesh=mesh,
        in_specs=(
            P("dp", "seq", None),
            P("dp", "seq", None),
            P(),
            P("seq", None),
            P("seq", None, None),
            P("seq", None, None),
        ),
        out_specs=(
            P("dp", "seq", None),
            P("dp", "seq", None),
            P(),
            P("seq", None),
            P("seq", None, None),
            P("seq", None, None),
        ),
        check_vma=False,
    )
```

profile of v0, /device:TPU:2, one launch (start us, length us, event | category | flops | bytes accessed | tf_op | source)
XLA Modules:
  0.0 599.1 jit_solution(1992488106284117112)
XLA Ops:
  7.9 68.7 %all-gather.2.cloned.1.call-done = bf16[1536,1536]{1,0:T(8,128)(2,1)} async-done(((bf16[48,1536]{1,0:T(8,128)(2,1)}), bf16[1536,1536]{1,0:T(8,128)(2,1)}) %all-gather.2.cloned.1.call-update) | async-done | bytes 4718608 | tf_op jit(solution)/shard_map/all_gather | solution.py:54
  76.6 7.6 %fusion.2 = (bf16[512,1536]{1,0:T(8,128)(2,1)S(1)}, f32[512,1536]{1,0:T(8,128)}) fusion(bf16[1,512,1536]{2,1,0:T(8,128)(2,1)} %param.7, bf16[1536,1536]{1,0:T(8,128)(2,1)} %all-gather.2.cloned.1.call-done, bf16[1,512,1536]{2,1,0:T(8,128)(2,1)} %param.6), kind=kOutput, calls=%fused_computation.9 | convolution fusion | flops 2418278400 | bytes 12582912 | tf_op jit(solution)/shard_map/dot_general | solution.py:55
  85.4 42.4 %all_to_all.63 = bf16[4,128,1536]{2,0,1:T(4,128)(2,1)S(1)} all-to-all(bf16[4,128,1536]{2,0,1:T(4,128)(2,1)S(1)} %copy.58), channel_id=1, replica_groups=mesh['seq'=32,'dp'=8] {'seq'}, dimensions={1} | all-to-all | bytes 3145728 | tf_op jit(solution)/shard_map/all_to_all | solution.py:61
  130.4 2.5 copy.61
  132.9 7.2 %all-to-all-start.3 = ((bf16[128,4,1536]{2,1,0:T(4,128)(2,1)}), bf16[128,4,1536]{2,1,0:T(4,128)(2,1)}, u32[]{:S(2)}, u32[]{:S(2)}) async-start(bf16[128,4,1536]{2,1,0:T(4,128)(2,1)} %copy.61), calls=%async_computation.3 | async-start | bytes 3145728 | tf_op jit(solution)/shard_map/all_to_all | solution.py:25
  143.0 6.2 %collective-permute-start.1 = (bf16[1,1536]{1,0:T(2,128)(2,1)S(1)}, bf16[1,1536]{1,0:T(2,128)(2,1)S(1)}, u32[]{:S(2)}, u32[]{:S(2)}) collective-permute-start(bf16[1,1536]{1,0:T(2,128)(2,1)S(1)} %get-tuple-element.42), channel_id=1, source_target_pairs={{8,0},{16,8},{24,16},{32,24},{40,32},{48,40},{56,48},{64,56},{72,6... | collective-permute-start | bytes 9224 | tf_op jit(solution)/shard_map/ppermute | solution.py:15
  149.3 20.2 %collective-permute-done = bf16[1,1536]{1,0:T(2,128)(2,1)S(1)} collective-permute-done((bf16[1,1536]{1,0:T(2,128)(2,1)S(1)}, bf16[1,1536]{1,0:T(2,128)(2,1)S(1)}, u32[]{:S(2)}, u32[]{:S(2)}) %collective-permute-start) | collective-permute-done | bytes 3104 | tf_op jit(solution)/shard_map/ppermute | solution.py:14
  171.4 5.5 all-to-all-done.3
  176.9 3.1 copy.62
  180.0 3.7 all_to_all.58
  183.7 2.6 fusion.9
  191.1 43.9 %all_to_all.64 = bf16[128,4,1536]{2,1,0:T(4,128)(2,1)S(1)} all-to-all(bf16[128,4,1536]{2,1,0:T(4,128)(2,1)S(1)} %copy.53), channel_id=1, replica_groups=mesh['seq'=32,'dp'=8] {'seq'}, dimensions={0} | all-to-all | bytes 3145728 | tf_op jit(solution)/shard_map/all_to_all | solution.py:25
  239.2 42.8 %all_to_all.65 = bf16[128,4,1536]{2,1,0:T(4,128)(2,1)S(1)} all-to-all(bf16[128,4,1536]{2,1,0:T(4,128)(2,1)S(1)} %copy.56), channel_id=1, replica_groups=mesh['seq'=32,'dp'=8] {'seq'}, dimensions={0} | all-to-all | bytes 3145728 | tf_op jit(solution)/shard_map/all_to_all | solution.py:25
  282.7 2.3 reshape.55
  284.9 9.1 %convolution_bitcast_fusion = f32[1536,1536]{0,1:T(8,128)} fusion(f32[1,512,1536]{2,1,0:T(8,128)} %reshape.55, bf16[1,512,1536]{2,1,0:T(8,128)(2,1)} %param.7, bf16[1,512,1536]{2,1,0:T(8,128)(2,1)} %param.6), kind=kOutput, calls=%fused_computation | convolution fusion | flops 2418278400 | bytes 15728640 | tf_op jit(solution)/shard_map/dot_general | solution.py:105
  294.1 9.6 %copy.70 = f32[1536,1536]{1,0:T(8,128)} copy(f32[1536,1536]{0,1:T(8,128)} %convolution_bitcast_fusion) | data formatting | bytes 18874368
  304.6 3.6 collective-permute-start.2
  308.2 4.7 collective-permute-start.3
  312.9 3.2 fusion.28
  316.1 75.9 %psum.28 = f32[3,1536]{1,0:T(4,128)} all-reduce(f32[3,1536]{1,0:T(4,128)S(1)} %pad_maximum_fusion), channel_id=1, replica_groups=mesh['seq'=32,'dp'=8] {'seq','dp'}, use_global_device_ids=true, to_apply=%region_3.0 | all-reduce | flops 4608 | bytes 36864 | tf_op jit(solution)/shard_map/psum | solution.py:114
  392.0 3.7 maximum_convert_fusion.1
  399.3 50.2 %reduce-scatter.4.cloned.1.call-done = f32[48,1536]{1,0:T(8,128)} async-done(((f32[1536,1536]{1,0:T(8,128)}), f32[48,1536]{1,0:T(8,128)}) %reduce-scatter.4.cloned.1.call-update) | async-done | bytes 294928
  451.7 9.8 %fusion.14 = bf16[1,512,1536]{2,1,0:T(8,128)(2,1)} fusion(bf16[1536,1536]{1,0:T(8,128)(2,1)} %all-gather.2.cloned.1.call-done, f32[514,1536]{1,0:T(8,128)} %maximum_convert_fusion.1, bf16[512,1536]{1,0:T(8,128)(2,1)S(1)} %bitcast.78, f32[512,1536]{1,0:T(8,128)} %reshape.52, bf16[1,512,1536]{2,1,0:T(8,128)(2,1)} %param.7, f32[1536]{0:T(1024)S(1)} %get-tuple-element.33, ...), kind=kOutput, calls=%fused_computation.31 | convolution fusion | flops 2424569856 | bytes 18892800 | tf_op jit(solution)/shard_map/dot_general | solution.py:100
  463.0 125.0 %all-reduce.3.cloned.1.call-done = (f32[48,1536]{0,1:T(8,128)}, f32[4,128,128]{2,1,0:T(8,128)}, f32[4,128,128]{2,1,0:T(8,128)}) async-done(((f32[48,1536]{0,1:T(8,128)}, f32[4,128,128]{2,1,0:T(8,128)}, f32[4,128,128]{2,1,0:T(8,128)}), (f32[48,1536]{0,1:T(8,128)}, f32[4,128,128]{2,1,0:T(8,128)}, f32[4,128,128]{2,1,0:T(8,128)})) %all-reduce.3.cloned.1.call-update) | async-done | bytes 819216 | tf_op jit(solution)/shard_map/psum | solution.py:113
  (66 shorter events, 31.7 us)
Async XLA Ops:
  7.2 176.5 %copy-start = (bf16[4,128,128]{2,1,0:T(8,128)(2,1)S(1)}, bf16[4,128,128]{2,1,0:T(8,128)(2,1)}, u32[]{:S(2)}) copy-start(bf16[4,128,128]{2,1,0:T(8,128)(2,1)} %param.10) | copy-start | bytes 393220
  7.2 69.4 %all-gather.2.cloned.1.call-start = ((), (), s32[]{:S(2)}) async-start(), calls=%async_computation.5 | async-start | bytes 4866048 | tf_op jit(solution)/shard_map/all_gather | solution.py:54
  127.8 1.9 copy-start.12
  128.5 1.1 copy-start.7
  132.9 16.3 %copy-start.14 = (f32[3,1536]{1,0:T(4,128)S(1)}, f32[3,1536]{1,0:T(4,128)}, u32[]{:S(2)}) copy-start(f32[3,1536]{1,0:T(4,128)} %param.8) | copy-start | bytes 55300
  132.9 44.0 %all-to-all-start.3 = ((bf16[128,4,1536]{2,1,0:T(4,128)(2,1)}), bf16[128,4,1536]{2,1,0:T(4,128)(2,1)}, u32[]{:S(2)}, u32[]{:S(2)}) async-start(bf16[128,4,1536]{2,1,0:T(4,128)(2,1)} %copy.61), calls=%async_computation.3 | async-start | bytes 3145728 | tf_op jit(solution)/shard_map/all_to_all | solution.py:25
  140.1 309.4 %reduce-scatter.4.cloned.1.call-start = ((), (), s32[]{:S(2)}) async-start(), calls=%async_computation.6 | async-start | bytes 9732096
  140.9 28.6 %collective-permute-start = (bf16[1,1536]{1,0:T(2,128)(2,1)S(1)}, bf16[1,1536]{1,0:T(2,128)(2,1)S(1)}, u32[]{:S(2)}, u32[]{:S(2)}) collective-permute-start(bf16[1,1536]{1,0:T(2,128)(2,1)S(1)} %get-tuple-element.41), channel_id=1, source_target_pairs={{0,8},{8,16},{16,24},{24,32},{32,40},{40,48},{48,56},{56,64},{64,7... | collective-permute-start | bytes 9224 | tf_op jit(solution)/shard_map/ppermute | solution.py:14
  143.0 26.5 %collective-permute-start.1 = (bf16[1,1536]{1,0:T(2,128)(2,1)S(1)}, bf16[1,1536]{1,0:T(2,128)(2,1)S(1)}, u32[]{:S(2)}, u32[]{:S(2)}) collective-permute-start(bf16[1,1536]{1,0:T(2,128)(2,1)S(1)} %get-tuple-element.42), channel_id=1, source_target_pairs={{8,0},{16,8},{24,16},{32,24},{40,32},{48,40},{56,48},{64,56},{72,6... | collective-permute-start | bytes 9224 | tf_op jit(solution)/shard_map/ppermute | solution.py:15
  183.7 2.6 copy-start.2
  186.3 1.6 copy-start.3
  187.9 1.2 copy-start.5
  235.8 1.2 copy-start.9
  303.8 284.3 %all-reduce.3.cloned.1.call-start = ((), (), s32[]{:S(2)}) async-start(), calls=%async_computation.7 | async-start | bytes 2621440 | tf_op jit(solution)/shard_map/psum | solution.py:113
  304.6 87.4 %collective-permute-start.2 = (bf16[1,1536]{1,0:T(2,128)(2,1)S(1)}, bf16[1,1536]{1,0:T(2,128)(2,1)S(1)}, u32[]{:S(2)}, u32[]{:S(2)}) collective-permute-start(bf16[1,1536]{1,0:T(2,128)(2,1)S(1)} %get-tuple-element.39), channel_id=1, source_target_pairs={{0,8},{8,16},{16,24},{24,32},{32,40},{40,48},{48,56},{56,64},{64,7... | collective-permute-start | bytes 9224 | tf_op jit(solution)/shard_map/ppermute | solution.py:14
  308.2 83.8 %collective-permute-start.3 = (bf16[1,1536]{1,0:T(2,128)(2,1)S(1)}, bf16[1,1536]{1,0:T(2,128)(2,1)S(1)}, u32[]{:S(2)}, u32[]{:S(2)}) collective-permute-start(bf16[1,1536]{1,0:T(2,128)(2,1)S(1)} %get-tuple-element.40), channel_id=1, source_target_pairs={{8,0},{16,8},{24,16},{32,24},{40,32},{48,40},{56,48},{64,56},{72,6... | collective-permute-start | bytes 9224 | tf_op jit(solution)/shard_map/ppermute | solution.py:15
  392.0 3.8 copy-start.8
  392.0 3.8 copy-start.10
  399.3 52.4 %copy-start.4 = (bf16[4,1536,128]{1,2,0:T(8,128)(2,1)S(1)}, bf16[4,1536,128]{1,2,0:T(8,128)(2,1)}, u32[]{:S(2)}) copy-start(bf16[4,1536,128]{1,2,0:T(8,128)(2,1)} %copy-done.3) | copy-start | bytes 4718596
  451.6 9.8 %copy-start.6 = (f32[512,1536]{1,0:T(8,128)S(1)}, f32[512,1536]{1,0:T(8,128)}, u32[]{:S(2)}) copy-start(f32[512,1536]{1,0:T(8,128)} %reshape.52) | copy-start | bytes 9437188
  451.7 9.8 %copy-start.11 = (f32[512,1536]{1,0:T(8,128)S(1)}, f32[512,1536]{1,0:T(8,128)}, u32[]{:S(2)}) copy-start(f32[512,1536]{1,0:T(8,128)} %get-tuple-element.44) | copy-start | bytes 9437188
  461.5 131.1 %copy-start.1 = (bf16[4,128,128]{2,1,0:T(8,128)(2,1)S(1)}, bf16[4,128,128]{2,1,0:T(8,128)(2,1)}, u32[]{:S(2)}) copy-start(bf16[4,128,128]{2,1,0:T(8,128)(2,1)} %param.10) | copy-start | bytes 393220
  588.0 3.8 copy-start.13
Sparse Core Ops, SparseCore 0:
  9.9 66.6 all-gather.1
  303.9 145.5 reduce-scatter.3
  452.9 135.0 all-reduce.2
where the time goes:
time: 600 us; the launch traced here: 599 us
  waiting for transfers between devices  270 us (45%)
  blocking collectives  205 us (34%)
  local copies, waits for them, and re-layouts  41 us (7%)
  matrix products  35.8 us (6%)
  starting transfers between devices  23.9 us (4%)
  between operations  14 us (2%)
  other arithmetic  9.23 us (2%)
    psum x1, waiting for transfers between devices, shards(): grad_gate = lax.psum(weight_part, 'dp')  125 us
    all_to_all x2, blocking collectives, regroup(): lax.all_to_all(values, 'seq', split_axis=0, concat_axis=1, tiled=True)  86.7 us
    psum x1, blocking collectives, shards(): grad_conv = lax.psum(conv_part, ('seq', 'dp'))  75.9 us
    all_gather x1, waiting for transfers between devices, shards(): whole_gate = lax.all_gather(gate_weight, 'seq', axis=0, tiled=True)  68.7 us
    unnamed x4, waiting for transfers between devices  50.9 us
    all_to_all x1, blocking collectives, shards(): lax.all_to_all(d_monarch.reshape(local_blocks, block_size, feat_width), '...  42.4 us
    ppermute x2, waiting for transfers between devices, with_halo(): before = lax.ppermute(last, axis, up)  20.2 us
    unnamed x35, local copies, waits for them, and re-layouts  19.9 us
  transfers between devices with their start and end apart: 8, of which 5 were waited for; matrix products, arithmetic and copies ran while one was open for 4% of the time, Pallas kernels for 0%

commit v1 on v0

--- a/solution.py
+++ b/solution.py
@@ -111,7 +111,7 @@
     )
     grad_first, trailing_factor_gradient = lax.psum((grad_first, trailing_factor_gradient), "dp")
     grad_gate = lax.psum(weight_part, "dp")
-    grad_conv = lax.psum(conv_part, ("seq", "dp"))
+    grad_conv = lax.psum(lax.psum(conv_part, "seq"), "dp")
     return (
         mixed[None],
         grad_tokens[None],

time: 600 us -> 637 us (1.062)
  blocking collectives: 205 us -> 297 us
  waiting for transfers between devices: 270 us -> 215 us
    psum x1 -> x2, blocking collectives: 75.9 us -> 168 us  [shards(): grad_conv = lax.psum(lax.psum(conv_part, 'seq'), 'dp')]
    unnamed x4, waiting for transfers between devices: 50.9 us -> 0.72 us
  transfers between devices with their start and end apart: 8 -> 8, of which waited for: 5 -> 4; matrix products, arithmetic and copies ran while one was open for 4% -> 4% of each run, Pallas kernels for 0% -> 0%
where the time goes in v1:
time: 637 us; the launch traced here: 636 us
  blocking collectives  297 us (47%)
  waiting for transfers between devices  215 us (34%)
  local copies, waits for them, and re-layouts  41 us (6%)
  matrix products  35.8 us (6%)
  starting transfers between devices  23.9 us (4%)
  between operations  14 us (2%)
  other arithmetic  9.21 us (1%)
    psum x2, blocking collectives, shards(): grad_conv = lax.psum(lax.psum(conv_part, 'seq'), 'dp')  168 us
    psum x1, waiting for transfers between devices, shards(): grad_gate = lax.psum(weight_part, 'dp')  120 us
    all_to_all x2, blocking collectives, regroup(): lax.all_to_all(values, 'seq', split_axis=0, concat_axis=1, tiled=True)  86.7 us
    all_gather x1, waiting for transfers between devices, shards(): whole_gate = lax.all_gather(gate_weight, 'seq', axis=0, tiled=True)  68.7 us
    all_to_all x1, blocking collectives, shards(): lax.all_to_all(d_monarch.reshape(local_blocks, block_size, feat_width), '...  42.4 us
    ppermute x2, waiting for transfers between devices, with_halo(): before = lax.ppermute(last, axis, up)  20.2 us
    unnamed x35, local copies, waits for them, and re-layouts  20 us
  transfers between devices with their start and end apart: 8, of which 4 were waited for; matrix products, arithmetic and copies ran while one was open for 4% of the time, Pallas kernels for 0%

profile of v1, /device:TPU:2, one launch (start us, length us, event | category | flops | bytes accessed | tf_op | source)
XLA Modules:
  0.0 636.2 jit_solution(4284799706685939097)
XLA Ops:
  7.9 68.7 %all-gather.2.cloned.1.call-done = bf16[1536,1536]{1,0:T(8,128)(2,1)} async-done(((bf16[48,1536]{1,0:T(8,128)(2,1)}), bf16[1536,1536]{1,0:T(8,128)(2,1)}) %all-gather.2.cloned.1.call-update) | async-done | bytes 4718608 | tf_op jit(solution)/shard_map/all_gather | solution.py:54
  76.6 7.6 %fusion.2 = (bf16[512,1536]{1,0:T(8,128)(2,1)S(1)}, f32[512,1536]{1,0:T(8,128)}) fusion(bf16[1,512,1536]{2,1,0:T(8,128)(2,1)} %param.7, bf16[1536,1536]{1,0:T(8,128)(2,1)} %all-gather.2.cloned.1.call-done, bf16[1,512,1536]{2,1,0:T(8,128)(2,1)} %param.6), kind=kOutput, calls=%fused_computation.9 | convolution fusion | flops 2418278400 | bytes 12582912 | tf_op jit(solution)/shard_map/dot_general | solution.py:55
  85.4 42.4 %all_to_all.63 = bf16[4,128,1536]{2,0,1:T(4,128)(2,1)S(1)} all-to-all(bf16[4,128,1536]{2,0,1:T(4,128)(2,1)S(1)} %copy.58), channel_id=1, replica_groups=mesh['seq'=32,'dp'=8] {'seq'}, dimensions={1} | all-to-all | bytes 3145728 | tf_op jit(solution)/shard_map/all_to_all | solution.py:61
  130.4 2.5 copy.61
  132.9 7.2 %all-to-all-start.3 = ((bf16[128,4,1536]{2,1,0:T(4,128)(2,1)}), bf16[128,4,1536]{2,1,0:T(4,128)(2,1)}, u32[]{:S(2)}, u32[]{:S(2)}) async-start(bf16[128,4,1536]{2,1,0:T(4,128)(2,1)} %copy.61), calls=%async_computation.3 | async-start | bytes 3145728 | tf_op jit(solution)/shard_map/all_to_all | solution.py:25
  143.0 6.2 collective-permute-start.1
  149.3 20.2 %collective-permute-done = bf16[1,1536]{1,0:T(2,128)(2,1)S(1)} collective-permute-done((bf16[1,1536]{1,0:T(2,128)(2,1)S(1)}, bf16[1,1536]{1,0:T(2,128)(2,1)S(1)}, u32[]{:S(2)}, u32[]{:S(2)}) %collective-permute-start) | collective-permute-done | bytes 3104 | tf_op jit(solution)/shard_map/ppermute | solution.py:14
  171.4 5.5 all-to-all-done.3
  176.9 3.1 copy.62
  180.0 3.7 all_to_all.58
  183.7 2.6 fusion.9
  191.1 43.9 %all_to_all.64 = bf16[128,4,1536]{2,1,0:T(4,128)(2,1)S(1)} all-to-all(bf16[128,4,1536]{2,1,0:T(4,128)(2,1)S(1)} %copy.53), channel_id=1, replica_groups=mesh['seq'=32,'dp'=8] {'seq'}, dimensions={0} | all-to-all | bytes 3145728 | tf_op jit(solution)/shard_map/all_to_all | solution.py:25
  239.2 42.8 %all_to_all.65 = bf16[128,4,1536]{2,1,0:T(4,128)(2,1)S(1)} all-to-all(bf16[128,4,1536]{2,1,0:T(4,128)(2,1)S(1)} %copy.56), channel_id=1, replica_groups=mesh['seq'=32,'dp'=8] {'seq'}, dimensions={0} | all-to-all | bytes 3145728 | tf_op jit(solution)/shard_map/all_to_all | solution.py:25
  284.9 9.2 %convolution_bitcast_fusion = f32[1536,1536]{0,1:T(8,128)} fusion(f32[1,512,1536]{2,1,0:T(8,128)} %reshape.55, bf16[1,512,1536]{2,1,0:T(8,128)(2,1)} %param.7, bf16[1,512,1536]{2,1,0:T(8,128)(2,1)} %param.6), kind=kOutput, calls=%fused_computation | convolution fusion | flops 2418278400 | bytes 15728640 | tf_op jit(solution)/shard_map/dot_general | solution.py:105
  294.1 9.6 %copy.70 = f32[1536,1536]{1,0:T(8,128)} copy(f32[1536,1536]{0,1:T(8,128)} %convolution_bitcast_fusion) | data formatting | bytes 18874368
  304.6 3.6 collective-permute-start.2
  308.3 4.7 collective-permute-start.3
  312.9 114.9 %psum.35 = f32[3,1536]{1,0:T(4,128)S(1)} all-reduce(f32[3,1536]{1,0:T(4,128)S(1)} %pad_maximum_fusion), channel_id=1, replica_groups=mesh['seq'=32,'dp'=8] {'seq'}, use_global_device_ids=true, to_apply=%region_3.0 | all-reduce | flops 4608 | bytes 36864 | tf_op jit(solution)/shard_map/psum | solution.py:114
  427.9 3.2 fusion.28
  431.1 52.8 %psum.36 = f32[3,1536]{1,0:T(4,128)} all-reduce(f32[3,1536]{1,0:T(4,128)S(1)} %psum.35), channel_id=1, replica_groups=mesh['seq'=32,'dp'=8] {'dp'}, use_global_device_ids=true, to_apply=%region_4.0 | all-reduce | flops 4608 | bytes 36864 | tf_op jit(solution)/shard_map/psum | solution.py:114
  483.9 3.7 maximum_convert_fusion.1
  491.2 2.3 copy.71
  493.5 9.8 %fusion.14 = bf16[1,512,1536]{2,1,0:T(8,128)(2,1)} fusion(bf16[1536,1536]{1,0:T(8,128)(2,1)} %all-gather.2.cloned.1.call-done, f32[514,1536]{1,0:T(8,128)} %maximum_convert_fusion.1, bf16[512,1536]{1,0:T(8,128)(2,1)S(1)} %bitcast.78, f32[512,1536]{1,0:T(8,128)} %reshape.52, bf16[1,512,1536]{2,1,0:T(8,128)(2,1)} %param.7, f32[1536]{0:T(1024)S(1)} %get-tuple-element.33, ...), kind=kOutput, calls=%fused_computation.31 | convolution fusion | flops 2424569856 | bytes 18892800 | tf_op jit(solution)/shard_map/dot_general | solution.py:100
  504.9 120.3 %all-reduce.3.cloned.1.call-done = (f32[48,1536]{0,1:T(8,128)}, f32[4,128,128]{2,1,0:T(8,128)}, f32[4,128,128]{2,1,0:T(8,128)}) async-done(((f32[48,1536]{0,1:T(8,128)}, f32[4,128,128]{2,1,0:T(8,128)}, f32[4,128,128]{2,1,0:T(8,128)}), (f32[48,1536]{0,1:T(8,128)}, f32[4,128,128]{2,1,0:T(8,128)}, f32[4,128,128]{2,1,0:T(8,128)})) %all-reduce.3.cloned.1.call-update) | async-done | bytes 819216 | tf_op jit(solution)/shard_map/psum | solution.py:113
  (67 shorter events, 31.7 us)
Async XLA Ops:
  7.2 176.5 %copy-start = (bf16[4,128,128]{2,1,0:T(8,128)(2,1)S(1)}, bf16[4,128,128]{2,1,0:T(8,128)(2,1)}, u32[]{:S(2)}) copy-start(bf16[4,128,128]{2,1,0:T(8,128)(2,1)} %param.10) | copy-start | bytes 393220
  7.2 69.4 %all-gather.2.cloned.1.call-start = ((), (), s32[]{:S(2)}) async-start(), calls=%async_computation.5 | async-start | bytes 4866048 | tf_op jit(solution)/shard_map/all_gather | solution.py:54
  127.8 1.9 copy-start.12
  128.6 1.1 copy-start.7
  132.9 16.3 %copy-start.14 = (f32[3,1536]{1,0:T(4,128)S(1)}, f32[3,1536]{1,0:T(4,128)}, u32[]{:S(2)}) copy-start(f32[3,1536]{1,0:T(4,128)} %param.8) | copy-start | bytes 55300
  132.9 44.0 %all-to-all-start.3 = ((bf16[128,4,1536]{2,1,0:T(4,128)(2,1)}), bf16[128,4,1536]{2,1,0:T(4,128)(2,1)}, u32[]{:S(2)}, u32[]{:S(2)}) async-start(bf16[128,4,1536]{2,1,0:T(4,128)(2,1)} %copy.61), calls=%async_computation.3 | async-start | bytes 3145728 | tf_op jit(solution)/shard_map/all_to_all | solution.py:25
  140.1 351.0 %reduce-scatter.4.cloned.1.call-start = ((), (), s32[]{:S(2)}) async-start(), calls=%async_computation.6 | async-start | bytes 9732096
  140.9 28.6 %collective-permute-start = (bf16[1,1536]{1,0:T(2,128)(2,1)S(1)}, bf16[1,1536]{1,0:T(2,128)(2,1)S(1)}, u32[]{:S(2)}, u32[]{:S(2)}) collective-permute-start(bf16[1,1536]{1,0:T(2,128)(2,1)S(1)} %get-tuple-element.41), channel_id=1, source_target_pairs={{0,8},{8,16},{16,24},{24,32},{32,40},{40,48},{48,56},{56,64},{64,7... | collective-permute-start | bytes 9224 | tf_op jit(solution)/shard_map/ppermute | solution.py:14
  143.0 26.5 %collective-permute-start.1 = (bf16[1,1536]{1,0:T(2,128)(2,1)S(1)}, bf16[1,1536]{1,0:T(2,128)(2,1)S(1)}, u32[]{:S(2)}, u32[]{:S(2)}) collective-permute-start(bf16[1,1536]{1,0:T(2,128)(2,1)S(1)} %get-tuple-element.42), channel_id=1, source_target_pairs={{8,0},{16,8},{24,16},{32,24},{40,32},{48,40},{56,48},{64,56},{72,6... | collective-permute-start | bytes 9224 | tf_op jit(solution)/shard_map/ppermute | solution.py:15
  183.7 2.6 copy-start.2
  186.3 1.6 copy-start.3
  187.9 1.1 copy-start.5
  235.9 1.2 copy-start.9
  303.8 321.3 %all-reduce.3.cloned.1.call-start = ((), (), s32[]{:S(2)}) async-start(), calls=%async_computation.7 | async-start | bytes 2621440 | tf_op jit(solution)/shard_map/psum | solution.py:113
  304.6 179.3 %collective-permute-start.2 = (bf16[1,1536]{1,0:T(2,128)(2,1)S(1)}, bf16[1,1536]{1,0:T(2,128)(2,1)S(1)}, u32[]{:S(2)}, u32[]{:S(2)}) collective-permute-start(bf16[1,1536]{1,0:T(2,128)(2,1)S(1)} %get-tuple-element.39), channel_id=1, source_target_pairs={{0,8},{8,16},{16,24},{24,32},{32,40},{40,48},{48,56},{56,64},{64,7... | collective-permute-start | bytes 9224 | tf_op jit(solution)/shard_map/ppermute | solution.py:14
  308.3 175.7 %collective-permute-start.3 = (bf16[1,1536]{1,0:T(2,128)(2,1)S(1)}, bf16[1,1536]{1,0:T(2,128)(2,1)S(1)}, u32[]{:S(2)}, u32[]{:S(2)}) collective-permute-start(bf16[1,1536]{1,0:T(2,128)(2,1)S(1)} %get-tuple-element.40), channel_id=1, source_target_pairs={{8,0},{16,8},{24,16},{32,24},{40,32},{48,40},{56,48},{64,56},{72,6... | collective-permute-start | bytes 9224 | tf_op jit(solution)/shard_map/ppermute | solution.py:15
  483.9 3.7 copy-start.8
  483.9 3.7 copy-start.10
  491.2 2.3 copy-start.4
  493.5 9.8 %copy-start.6 = (f32[512,1536]{1,0:T(8,128)S(1)}, f32[512,1536]{1,0:T(8,128)}, u32[]{:S(2)}) copy-start(f32[512,1536]{1,0:T(8,128)} %reshape.52) | copy-start | bytes 9437188
  493.5 9.8 %copy-start.11 = (f32[512,1536]{1,0:T(8,128)S(1)}, f32[512,1536]{1,0:T(8,128)}, u32[]{:S(2)}) copy-start(f32[512,1536]{1,0:T(8,128)} %get-tuple-element.44) | copy-start | bytes 9437188
  503.3 126.4 %copy-start.1 = (bf16[4,128,128]{2,1,0:T(8,128)(2,1)S(1)}, bf16[4,128,128]{2,1,0:T(8,128)(2,1)}, u32[]{:S(2)}) copy-start(bf16[4,128,128]{2,1,0:T(8,128)(2,1)} %param.10) | copy-start | bytes 393220
  625.1 3.8 copy-start.13
Sparse Core Ops, SparseCore 0:
  9.9 66.6 all-gather.1
  303.9 146.2 reduce-scatter.3
  493.6 131.4 all-reduce.2
